TPU v7x, 32 devices: a whole 2x2x4 slice. The times are simulated.
32 devices in a mesh: ens: 8 (over z, x), mesh: 4 (over y, core).
Axes of the slice: x: 2, y: 2, z: 4, core: 2. Of those that a mesh axis runs over, the one named last changes fastest.
Arguments:
- inputs: bfloat16 [8, 1024, 512], P('ens', 'mesh'), may hold values from -6 to 6
- cotangent: bfloat16 [8, 1024, 512], P('ens', 'mesh'), may hold values from -6 to 6
- noise_level: float32 [8], P('ens'), may hold values from 0.02 to 80
- neighbours: int32 [1024, 32], P('mesh'), may hold values from 0 to 1023, as said below
- live_slots: int32 [1024, 32], P('mesh'), may hold values from 0 to 1
- projections: bfloat16 [2, 4, 512, 512], replicated, may hold values from -4 to 4
- film_weights: float32 [2, 32, 1024], replicated, may hold values from -0.5 to 0.5
Outputs:
- grad_input: bfloat16 [8, 1024, 512], P('ens', 'mesh')
- grad_projections: float32 [2, 4, 512, 512], P(None, None, 'ens', 'mesh')
- grad_film: float32 [2, 32, 1024], P(None, None, 'mesh')
Inputs may be any that keep to these rules, and one draw needn't show every extreme that they name: `neighbours`: slot 0 of node i names i and is live. The live slots of a node name distinct nodes within 128 of it; every node at least 128 from both ends of the numbering has a live slot exactly 128 away. Padded slots name the node itself.
All inputs are finite; a program needn't handle non-finite values.
Results may differ from a plain program's by a relative error of at most 0.028.
Values may be sent and summed in bfloat16 or wider, within the bound.
No kernel may reach another device: no remote copies, remote signals or barrier semaphores. Data moves between devices by JAX's collectives and lax.ppermute only.
A program may use at most 64 MiB of HBM per device.

v0:
```python
import math
import jax
import jax.numpy as jnp
from jax import lax
from jax.sharding import PartitionSpec as P

HEADS = 4
NOISE_FREQ = 16
LAYERS = 2
epsilon = 1e-05


def padded(cells, sides, width):
    for axis, dim in sides:
        count = lax.axis_size(axis)
        ends = count - 1
        head = lax.slice_in_dim(cells, 0, width, axis=dim)
        tail = lax.slice_in_dim(cells, cells.shape[dim] - width, cells.shape[dim], axis=dim)
        cells = jnp.concatenate(
            [
                lax.ppermute(tail, axis, [(i, (i + 1) % count) for i in range(ends)]),
                cells,
                lax.ppermute(head, axis, [((i + 1) % count, i) for i in range(ends)]),
            ],
            axis=dim,
        )
    return cells


def from_behind(block, axis, distance):
    devices = range(lax.axis_size(axis))
    route = [(i - distance, i) for i in devices if i - distance in devices]
    return lax.ppermute(block, axis, route)


def noise_features(noise_level):
    frequency = jnp.arange(1, NOISE_FREQ + 1).astype(jnp.float32)
    angles = jnp.log(noise_level)[:, None] * frequency[None, :]
    return jnp.concatenate([jnp.sin(angles), jnp.cos(angles)], axis=1)


def project(left_side, right_side):
    return jnp.dot(left_side, right_side, preferred_element_type=jnp.float32)


def contract_rows(left_side, right_side):
    return lax.dot_general(
        left_side, right_side, (((0,), (0,)), ((), ())), preferred_element_type=jnp.float32
    )


def contract_cols(left_side, right_side):
    return lax.dot_general(
        left_side, right_side, (((1,), (1,)), ((), ())), preferred_element_type=jnp.float32
    )


def normalize(states, film_row, model_width):
    values = states.astype(jnp.float32)
    centre = jnp.mean(values, axis=1, keepdims=True)
    spread = jnp.mean(jnp.square(values - centre), axis=1, keepdims=True)
    inverse = lax.rsqrt(spread + epsilon)
    unit_rows = (values - centre) * inverse
    normed = (unit_rows * (1.0 + film_row[:model_width]) + film_row[model_width:]).astype(
        jnp.bfloat16
    )
    return (unit_rows, inverse, normed)


def dense_attention(query_head, key_head, present, head_size):
    scores = contract_cols(query_head, key_head) / math.sqrt(head_size)
    scores = jnp.where(present, scores, -jnp.inf)
    row_peak = jnp.max(scores, axis=1, keepdims=True)
    weights = jnp.where(present, jnp.exp(scores - row_peak), 0.0)
    return weights / jnp.sum(weights, axis=1, keepdims=True)


def extend_rims(normed, weights, rim_width, model_width):
    joined = jnp.concatenate(
        [
            project(normed, weights[1]).astype(jnp.bfloat16),
            project(normed, weights[2]).astype(jnp.bfloat16),
        ],
        axis=1,
    )
    joined_ext = padded(joined, (("mesh", 0),), rim_width)
    key_ext = joined_ext[:, :model_width]
    value_ext = joined_ext[:, model_width:]
    return (key_ext, value_ext)


def body(inputs, cotangent, noise_level, neighbours, live_slots, projections, film_weights):
    current = inputs[0]
    node_count, model_width = current.shape
    head_size = model_width // HEADS
    rim_width = node_count // 2
    window = node_count + 2 * rim_width
    offset = lax.axis_index("mesh") * node_count - rim_width
    columns = neighbours - offset
    row_ids = jnp.broadcast_to(jnp.arange(node_count, dtype=jnp.int32)[:, None], columns.shape)
    adjacency = (
        jnp.zeros((node_count, window), jnp.float32)
        .at[row_ids, columns]
        .add(live_slots.astype(jnp.float32))
    )
    present = adjacency > 0.5
    embedding = noise_features(noise_level)[0]
    film_rows = [
        jnp.dot(embedding[None, :], film_weights[layer_number], precision=lax.Precision.HIGHEST)[0]
        for layer_number in range(LAYERS)
    ]
    stored = []
    for layer_number in range(LAYERS):
        weights = projections[layer_number]
        unit_rows, inverse, normed = normalize(current, film_rows[layer_number], model_width)
        queries = project(normed, weights[0]).astype(jnp.bfloat16)
        key_ext, value_ext = extend_rims(normed, weights, rim_width, model_width)
        pieces = []
        for head_index in range(HEADS):
            head_cols = slice(head_index * head_size, (head_index + 1) * head_size)
            attention = dense_attention(
                queries[:, head_cols], key_ext[:, head_cols], present, head_size
            )
            pieces.append(project(attention.astype(jnp.bfloat16), value_ext[:, head_cols]))
        attended = jnp.concatenate(pieces, axis=1).astype(jnp.bfloat16)
        stored.append((unit_rows, inverse, normed, queries, key_ext, value_ext, attended))
        current = (current.astype(jnp.float32) + project(attended, weights[3])).astype(jnp.bfloat16)
    upstream = cotangent[0]
    weight_list = [None] * LAYERS
    film_list = [None] * LAYERS
    for layer_number in reversed(range(LAYERS)):
        weights = projections[layer_number]
        film_row = film_rows[layer_number]
        unit_rows, inverse, normed, queries, key_ext, value_ext, attended = stored[layer_number]
        grad_out = contract_rows(attended, upstream)
        grad_attended = contract_cols(upstream, weights[3]).astype(jnp.bfloat16)
        query_parts, key_parts, value_parts = ([], [], [])
        for head_index in range(HEADS):
            head_cols = slice(head_index * head_size, (head_index + 1) * head_size)
            attention = dense_attention(
                queries[:, head_cols], key_ext[:, head_cols], present, head_size
            )
            rounded = attention.astype(jnp.bfloat16)
            grad_head = grad_attended[:, head_cols]
            grad_probs = contract_cols(grad_head, value_ext[:, head_cols])
            grad_scores = (
                attention
                * (grad_probs - jnp.sum(attention * grad_probs, axis=1, keepdims=True))
                / math.sqrt(head_size)
            ).astype(jnp.bfloat16)
            query_parts.append(project(grad_scores, key_ext[:, head_cols]))
            key_parts.append(contract_rows(grad_scores, queries[:, head_cols]))
            value_parts.append(contract_rows(rounded, grad_head))
        grad_queries = jnp.concatenate(query_parts, axis=1).astype(jnp.bfloat16)
        rim_terms = jnp.concatenate(key_parts + value_parts, axis=1)
        from_above = from_behind(rim_terms[:rim_width].astype(jnp.bfloat16), "mesh", -1).astype(
            jnp.float32
        )
        from_below = from_behind(
            rim_terms[rim_width + node_count :].astype(jnp.bfloat16), "mesh", 1
        ).astype(jnp.float32)
        owned_rows = rim_terms[rim_width : rim_width + node_count]
        owned_rows = (
            owned_rows
            + jnp.pad(from_below, ((0, node_count - rim_width), (0, 0)))
            + jnp.pad(from_above, ((node_count - rim_width, 0), (0, 0)))
        )
        grad_keys = owned_rows[:, :model_width].astype(jnp.bfloat16)
        grad_values = owned_rows[:, model_width:].astype(jnp.bfloat16)
        weight_list[layer_number] = jnp.stack(
            [
                contract_rows(normed, grad_queries),
                contract_rows(normed, grad_keys),
                contract_rows(normed, grad_values),
                grad_out,
            ]
        )
        grad_normed = (
            contract_cols(grad_queries, weights[0])
            + contract_cols(grad_keys, weights[1])
            + contract_cols(grad_values, weights[2])
        )
        grad_conditioning = jnp.concatenate(
            [jnp.sum(grad_normed * unit_rows, axis=0), jnp.sum(grad_normed, axis=0)]
        )
        film_list[layer_number] = embedding[:, None] * grad_conditioning[None, :]
        grad_unit = grad_normed * (1.0 + film_row[:model_width])
        centred = (
            grad_unit
            - jnp.mean(grad_unit, axis=1, keepdims=True)
            - unit_rows * jnp.mean(grad_unit * unit_rows, axis=1, keepdims=True)
        )
        upstream = (upstream.astype(jnp.float32) + inverse * centred).astype(jnp.bfloat16)
    weight_grads = jnp.stack(weight_list)
    film_grads = jnp.stack(film_list)
    weight_part = lax.psum_scatter(
        weight_grads.astype(jnp.bfloat16), "ens", scatter_dimension=2, tiled=True
    )
    film_part = lax.psum(film_grads.astype(jnp.bfloat16), "ens")
    weight_out, film_out = (
        lax.psum_scatter(weight_part, "mesh", scatter_dimension=3, tiled=True).astype(jnp.float32),
        lax.psum_scatter(film_part, "mesh", scatter_dimension=2, tiled=True).astype(jnp.float32),
    )
    return (upstream[None], weight_out, film_out)


def solution(mesh):
    placed = (
        P("ens", "mesh", None),
        P("ens", "mesh", None),
        P("ens"),
        P("mesh", None),
        P("mesh", None),
        P(),
        P(),
    )
    return jax.shard_map(
        body,
        mesh=mesh,
        in_specs=placed,
        out_specs=(P("ens", "mesh", None), P(None, None, "ens", "mesh"), P(None, None, "mesh")),
        check_vma=False,
    )
```

profile of v0, /device:TPU:0, one launch (start us, length us, event | category | flops | bytes accessed | tf_op | source)
XLA Modules:
  0.0 294.2 jit_solution(6089208120001934512)
XLA Ops:
  8.0 1.1 convert_reduce_fusion
  9.1 1.2 fusion.37
  10.2 1.1 fusion.115
  11.5 1.6 convolution_convert_fusion.14
  13.1 1.4 convolution_convert_fusion.13
  14.5 2.4 collective-permute-start
  17.0 1.3 collective-permute-start.1
  19.1 56.7 %scatter_custom_fusion = f32[131072]{0:T(1024)S(1)} fusion(s32[8192]{0:T(1024)S(1)} %reshape.328, f32[8192]{0:T(1024)S(1)} %reshape.330, f32[]{:T(128)} %constant.46.clone.1), kind=kCustom, calls=%fused_computation.217 | custom fusion | flops 8192 | bytes 524292
  76.1 1.4 convolution_convert_fusion.15
  79.0 0.7 fusion.75
  83.4 5.1 %collective-permute-start.2 = (bf16[128,1024]{1,0:T(8,128)(2,1)S(1)}, bf16[128,1024]{1,0:T(8,128)(2,1)S(1)}, u32[]{:S(2)}, u32[]{:S(2)}) collective-permute-start(bf16[128,1024]{1,0:T(8,128)(2,1)S(1)} %get-tuple-element.31), channel_id=1, source_target_pairs={{0,1},{1,2},{2,3},{4,5},{5,6},{6,7},{8,9},{9,10},{10,11},{12,13},{... | collective-permute-start | bytes 786440 | tf_op jit(solution)/shard_map/ppermute | solution.py:21
  88.6 1.5 collective-permute-start.3
  90.7 2.5 collective-permute-done.3
  96.1 0.9 multiply_reduce_fusion.9
  101.5 6.7 %collective-permute-start.4 = (bf16[128,1024]{0,1:T(8,128)(2,1)S(1)}, bf16[128,1024]{0,1:T(8,128)(2,1)S(1)}, u32[]{:S(2)}, u32[]{:S(2)}) collective-permute-start(bf16[128,1024]{0,1:T(8,128)(2,1)S(1)} %get-tuple-element.29), channel_id=1, source_target_pairs={{0,1},{1,2},{2,3},{4,5},{5,6},{6,7},{8,9},{9,10},{10,11},{12,13},{... | collective-permute-start | bytes 786440 | tf_op jit(solution)/shard_map/ppermute | solution.py:33
  108.2 1.3 collective-permute-start.5
  110.5 1.1 collective-permute-done.5
  118.9 6.2 %collective-permute-start.6 = (bf16[128,1024]{0,1:T(8,128)(2,1)S(1)}, bf16[128,1024]{0,1:T(8,128)(2,1)S(1)}, u32[]{:S(2)}, u32[]{:S(2)}) collective-permute-start(bf16[128,1024]{0,1:T(8,128)(2,1)S(1)} %get-tuple-element.27), channel_id=1, source_target_pairs={{0,1},{1,2},{2,3},{4,5},{5,6},{6,7},{8,9},{9,10},{10,11},{12,13},{... | collective-permute-start | bytes 786440 | tf_op jit(solution)/shard_map/ppermute | solution.py:33
  125.1 1.5 collective-permute-start.7
  127.8 0.8 collective-permute-done.7
  130.0 2.3 pad_maximum_fusion
  132.4 1.4 fusion.56
  133.8 1.4 convolution_add_fusion.1
  135.2 1.6 fusion.36
  137.7 87.3 %reduce-scatter.6.cloned.1.call-done = bf16[2,4,64,512]{3,2,1,0:T(8,128)(2,1)} async-done(((bf16[2,4,512,512]{3,2,1,0:T(8,128)(2,1)}), bf16[2,4,64,512]{3,2,1,0:T(8,128)(2,1)}) %reduce-scatter.6.cloned.1.call-update) | async-done | bytes 524304 | tf_op jit(solution)/shard_map/reduce_scatter | solution.py:196
  224.9 1.6 copy.13
  226.6 1.4 reshape.338
  228.0 1.0 fusion.93
  229.0 18.3 %reduce-scatter.8.cloned.1.call-done = bf16[2,32,256]{2,1,0:T(8,128)(2,1)} async-done(((bf16[2,32,1024]{2,1,0:T(8,128)(2,1)}), bf16[2,32,256]{2,1,0:T(8,128)(2,1)}) %reduce-scatter.8.cloned.1.call-update) | async-done | bytes 32784 | tf_op jit(solution)/shard_map/reduce_scatter | solution.py:202
  247.3 37.8 %psum.8 = bf16[2,32,256]{2,1,0:T(8,128)(2,1)S(1)} all-reduce(bf16[2,32,256]{2,1,0:T(8,128)(2,1)} %reduce-scatter.8.cloned.1.call-done), channel_id=1, replica_groups=mesh['ens'=8,'mesh'=4] {'ens'}, use_global_device_ids=true, to_apply=%region_39.40 | all-reduce | flops 16384 | bytes 65536 | tf_op jit(solution)/shard_map/psum | solution.py:199
  285.7 1.1 reshape.339
  287.0 0.7 convert_element_type.206
  (148 shorter events, 26.5 us)
Async XLA Ops:
  7.2 5.9 %copy-start = (bf16[1,256,512]{2,1,0:T(8,128)(2,1)S(1)}, bf16[1,256,512]{2,1,0:T(8,128)(2,1)}, u32[]{:S(2)}) copy-start(bf16[1,256,512]{2,1,0:T(8,128)(2,1)} %param.7) | copy-start | bytes 786436
  7.2 217.8 %reduce-scatter.6.cloned.1.call-start = ((), (), s32[]{:S(2)}) async-start(), calls=%async_computation.3 | async-start | bytes 4718592 | tf_op jit(solution)/shard_map/reduce_scatter | solution.py:196
  11.4 6.8 %copy-start.2 = (f32[2,32,1024]{2,1,0:T(8,128)S(1)}, f32[2,32,1024]{2,1,0:T(8,128)}, u32[]{:S(2)}) copy-start(f32[2,32,1024]{2,1,0:T(8,128)} %param.13) | copy-start | bytes 786436
  11.4 7.1 %copy-start.4 = (s32[256,32]{0,1:T(8,128)S(1)}, s32[256,32]{0,1:T(8,128)}, u32[]{:S(2)}) copy-start(s32[256,32]{0,1:T(8,128)} %param.10) | copy-start | bytes 98308
  11.4 7.1 %copy-start.7 = (s32[2]{0:T(128)S(1)}, s32[2]{0:T(128)}, u32[]{:S(2)}) copy-start(s32[2]{0:T(128)} %constant.74) | copy-start | bytes 28
  11.4 7.2 %copy-start.6 = (s32[2]{0:T(128)S(1)}, s32[2]{0:T(128)}, u32[]{:S(2)}) copy-start(s32[2]{0:T(128)} %constant.71) | copy-start | bytes 28
  11.5 7.3 %copy-start.5 = (s32[256,32]{0,1:T(8,128)S(1)}, s32[256,32]{0,1:T(8,128)}, u32[]{:S(2)}) copy-start(s32[256,32]{0,1:T(8,128)} %param.11) | copy-start | bytes 98308
  14.5 63.0 %collective-permute-start = (bf16[128,1024]{1,0:T(8,128)(2,1)S(1)}, bf16[128,1024]{1,0:T(8,128)(2,1)S(1)}, u32[]{:S(2)}, u32[]{:S(2)}) collective-permute-start(bf16[128,1024]{1,0:T(8,128)(2,1)S(1)} %get-tuple-element.33), channel_id=1, source_target_pairs={{0,1},{1,2},{2,3},{4,5},{5,6},{6,7},{8,9},{9,10},{10,11},{12,13},{... | collective-permute-start | bytes 786440 | tf_op jit(solution)/shard_map/ppermute | solution.py:21
  17.0 60.6 %collective-permute-start.1 = (bf16[128,1024]{1,0:T(8,128)(2,1)S(1)}, bf16[128,1024]{1,0:T(8,128)(2,1)S(1)}, u32[]{:S(2)}, u32[]{:S(2)}) collective-permute-start(bf16[128,1024]{1,0:T(8,128)(2,1)S(1)} %get-tuple-element.34), channel_id=1, source_target_pairs={{1,0},{2,1},{3,2},{5,4},{6,5},{7,6},{9,8},{10,9},{11,10},{13,12},{... | collective-permute-start | bytes 786440 | tf_op jit(solution)/shard_map/ppermute | solution.py:23
  79.7 2.2 copy-start.1
  82.5 7.5 %copy-start.3 = (bf16[1,256,512]{2,1,0:T(8,128)(2,1)S(1)}, bf16[1,256,512]{2,1,0:T(8,128)(2,1)}, u32[]{:S(2)}) copy-start(bf16[1,256,512]{2,1,0:T(8,128)(2,1)} %param.8) | copy-start | bytes 786436
  83.4 7.3 %collective-permute-start.2 = (bf16[128,1024]{1,0:T(8,128)(2,1)S(1)}, bf16[128,1024]{1,0:T(8,128)(2,1)S(1)}, u32[]{:S(2)}, u32[]{:S(2)}) collective-permute-start(bf16[128,1024]{1,0:T(8,128)(2,1)S(1)} %get-tuple-element.31), channel_id=1, source_target_pairs={{0,1},{1,2},{2,3},{4,5},{5,6},{6,7},{8,9},{9,10},{10,11},{12,13},{... | collective-permute-start | bytes 786440 | tf_op jit(solution)/shard_map/ppermute | solution.py:21
  88.6 4.7 %collective-permute-start.3 = (bf16[128,1024]{1,0:T(8,128)(2,1)S(1)}, bf16[128,1024]{1,0:T(8,128)(2,1)S(1)}, u32[]{:S(2)}, u32[]{:S(2)}) collective-permute-start(bf16[128,1024]{1,0:T(8,128)(2,1)S(1)} %get-tuple-element.32), channel_id=1, source_target_pairs={{1,0},{2,1},{3,2},{5,4},{6,5},{7,6},{9,8},{10,9},{11,10},{13,12},{... | collective-permute-start | bytes 786440 | tf_op jit(solution)/shard_map/ppermute | solution.py:23
  101.5 9.0 %collective-permute-start.4 = (bf16[128,1024]{0,1:T(8,128)(2,1)S(1)}, bf16[128,1024]{0,1:T(8,128)(2,1)S(1)}, u32[]{:S(2)}, u32[]{:S(2)}) collective-permute-start(bf16[128,1024]{0,1:T(8,128)(2,1)S(1)} %get-tuple-element.29), channel_id=1, source_target_pairs={{0,1},{1,2},{2,3},{4,5},{5,6},{6,7},{8,9},{9,10},{10,11},{12,13},{... | collective-permute-start | bytes 786440 | tf_op jit(solution)/shard_map/ppermute | solution.py:33
  108.2 3.4 %collective-permute-start.5 = (bf16[128,1024]{0,1:T(8,128)(2,1)S(1)}, bf16[128,1024]{0,1:T(8,128)(2,1)S(1)}, u32[]{:S(2)}, u32[]{:S(2)}) collective-permute-start(bf16[128,1024]{0,1:T(8,128)(2,1)S(1)} %get-tuple-element.30), channel_id=1, source_target_pairs={{1,0},{2,1},{3,2},{5,4},{6,5},{7,6},{9,8},{10,9},{11,10},{13,12},{... | collective-permute-start | bytes 786440 | tf_op jit(solution)/shard_map/ppermute | solution.py:33
  118.9 8.8 %collective-permute-start.6 = (bf16[128,1024]{0,1:T(8,128)(2,1)S(1)}, bf16[128,1024]{0,1:T(8,128)(2,1)S(1)}, u32[]{:S(2)}, u32[]{:S(2)}) collective-permute-start(bf16[128,1024]{0,1:T(8,128)(2,1)S(1)} %get-tuple-element.27), channel_id=1, source_target_pairs={{0,1},{1,2},{2,3},{4,5},{5,6},{6,7},{8,9},{9,10},{10,11},{12,13},{... | collective-permute-start | bytes 786440 | tf_op jit(solution)/shard_map/ppermute | solution.py:33
  125.1 3.4 %collective-permute-start.7 = (bf16[128,1024]{0,1:T(8,128)(2,1)S(1)}, bf16[128,1024]{0,1:T(8,128)(2,1)S(1)}, u32[]{:S(2)}, u32[]{:S(2)}) collective-permute-start(bf16[128,1024]{0,1:T(8,128)(2,1)S(1)} %get-tuple-element.28), channel_id=1, source_target_pairs={{1,0},{2,1},{3,2},{5,4},{6,5},{7,6},{9,8},{10,9},{11,10},{13,12},{... | collective-permute-start | bytes 786440 | tf_op jit(solution)/shard_map/ppermute | solution.py:33
  132.3 115.0 %reduce-scatter.8.cloned.1.call-start = ((), (), s32[]{:S(2)}) async-start(), calls=%async_computation.4 | async-start | bytes 163840 | tf_op jit(solution)/shard_map/reduce_scatter | solution.py:202
  137.6 148.1 %reduce-scatter.10.cloned.1.call-start = ((), (), s32[]{:S(2)}) async-start(), calls=%async_computation.5 | async-start | bytes 655360
Sparse Core Ops, SparseCore 0:
  132.4 92.4 reduce-scatter.5
  227.9 19.2 reduce-scatter.7
  249.8 21.6 reduce-scatter.9
where the time goes:
time: 295 us; the launch traced here: 294 us
  waiting for transfers between devices  110 us (37%)
  other arithmetic  69.8 us (24%)
  blocking collectives  37.8 us (13%)
  matrix products  29.4 us (10%)
  starting transfers between devices  26.1 us (9%)
  between operations  15.4 us (5%)
  local copies, waits for them, and re-layouts  5.72 us (2%)
    reduce_scatter x1, waiting for transfers between devices, body(): lax.psum_scatter(weight_grads.astype(jnp.bfloat16), 'ens', scatter_dimens...  87.3 us
    unnamed x4, other arithmetic  56.9 us
    psum x1, blocking collectives, body(): film_part = lax.psum(film_grads.astype(jnp.bfloat16), 'ens')  37.8 us
    reduce_scatter x1, waiting for transfers between devices, body(): lax.psum_scatter(film_part, 'mesh', scatter_dimension=2, tiled=True)  18.3 us
    ppermute x4, starting transfers between devices, from_behind(): return lax.ppermute(block, axis, route)  15.7 us
    dot_general x24, matrix products, contract_cols(): lax.dot_general(left_side, right_side, (((1,), (1,)), ((), ())), preferre...  11.8 us
    dot_general x23, matrix products, project(): return jnp.dot(left_side, right_side, preferred_element_type=jnp.float32)  9.49 us
    ppermute x2, starting transfers between devices, padded(): lax.ppermute(tail, axis, [(i, (i + 1) % count) for i in range(ends)])  7.55 us
  transfers between devices with their start and end apart: 11, of which 5 were waited for; matrix products, arithmetic and copies ran while one was open for 24% of the time, Pallas kernels for 0%

commit v1 on v0

--- a/solution.py
+++ b/solution.py
@@ -196,7 +196,9 @@
     weight_part = lax.psum_scatter(
         weight_grads.astype(jnp.bfloat16), "ens", scatter_dimension=2, tiled=True
     )
-    film_part = lax.psum(film_grads.astype(jnp.bfloat16), "ens")
+    part = film_grads.astype(jnp.bfloat16)
+    parts = lax.all_gather(part, "ens")
+    film_part = jnp.sum(parts, axis=0)
     weight_out, film_out = (
         lax.psum_scatter(weight_part, "mesh", scatter_dimension=3, tiled=True).astype(jnp.float32),
         lax.psum_scatter(film_part, "mesh", scatter_dimension=2, tiled=True).astype(jnp.float32),

time: 295 us -> 325 us (1.10)
  waiting for transfers between devices: 110 us -> 171 us
  blocking collectives: 37.8 us -> 0 us
    psum x1 -> x0, blocking collectives: 37.8 us -> none  [body(): film_part = lax.psum(film_grads.astype(jnp.bfloat16), 'ens')]
    all_gather x0 -> x1, waiting for transfers between devices: none -> 35.8 us  [body(): parts = lax.all_gather(part, 'ens')]
    unnamed x4 -> x5, waiting for transfers between devices: 0.05 us -> 22.7 us
  transfers between devices with their start and end apart: 11 -> 12, of which waited for: 5 -> 7; matrix products, arithmetic and copies ran while one was open for 24% -> 24% of each run, Pallas kernels for 0% -> 0%
where the time goes in v1:
time: 325 us; the launch traced here: 324 us
  waiting for transfers between devices  171 us (53%)
  other arithmetic  72.8 us (22%)
  matrix products  32.4 us (10%)
  starting transfers between devices  26.2 us (8%)
  between operations  15.7 us (5%)
  local copies, waits for them, and re-layouts  5.86 us (2%)
    reduce_scatter x1, waiting for transfers between devices, body(): lax.psum_scatter(weight_grads.astype(jnp.bfloat16), 'ens', scatter_dimens...  88.5 us
    unnamed x4, other arithmetic  56.9 us
    all_gather x1, waiting for transfers between devices, body(): parts = lax.all_gather(part, 'ens')  35.8 us
    unnamed x5, waiting for transfers between devices  22.7 us
    reduce_scatter x1, waiting for transfers between devices, body(): lax.psum_scatter(film_part, 'mesh', scatter_dimension=2, tiled=True)  18.2 us
    ppermute x4, starting transfers between devices, from_behind(): return lax.ppermute(block, axis, route)  15.5 us
    dot_general x23, matrix products, project(): return jnp.dot(left_side, right_side, preferred_element_type=jnp.float32)  11.4 us
    dot_general x24, matrix products, contract_cols(): lax.dot_general(left_side, right_side, (((1,), (1,)), ((), ())), preferre...  10.9 us
  transfers between devices with their start and end apart: 12, of which 7 were waited for; matrix products, arithmetic and copies ran while one was open for 24% of the time, Pallas kernels for 0%

profile of v1, /device:TPU:0, one launch (start us, length us, event | category | flops | bytes accessed | tf_op | source)
XLA Modules:
  0.0 324.4 jit_solution(3812214077521883231)
XLA Ops:
  8.0 1.1 convert_reduce_fusion
  9.1 1.2 fusion.37
  10.2 1.1 fusion.115
  11.5 1.6 convolution_convert_fusion.14
  13.1 1.4 convolution_convert_fusion.13
  14.6 2.4 collective-permute-start
  17.0 1.3 collective-permute-start.1
  19.2 1.4 convolution_convert_fusion.9
  20.6 56.7 %scatter_custom_fusion = f32[131072]{0:T(1024)S(1)} fusion(s32[8192]{0:T(1024)S(1)} %reshape.389, f32[8192]{0:T(1024)S(1)} %reshape.391, f32[]{:T(128)} %constant.47.clone.1), kind=kCustom, calls=%fused_computation.217 | custom fusion | flops 8192 | bytes 524292
  77.6 1.4 convolution_convert_fusion.15
  85.0 5.2 %collective-permute-start.2 = (bf16[128,1024]{1,0:T(8,128)(2,1)S(1)}, bf16[128,1024]{1,0:T(8,128)(2,1)S(1)}, u32[]{:S(2)}, u32[]{:S(2)}) collective-permute-start(bf16[128,1024]{1,0:T(8,128)(2,1)S(1)} %get-tuple-element.31), channel_id=1, source_target_pairs={{0,1},{1,2},{2,3},{4,5},{5,6},{6,7},{8,9},{9,10},{10,11},{12,13},{... | collective-permute-start | bytes 786440 | tf_op jit(solution)/shard_map/ppermute | solution.py:21
  90.1 1.5 collective-permute-start.3
  92.0 2.8 collective-permute-done.3
  104.5 6.7 %collective-permute-start.4 = (bf16[128,1024]{0,1:T(8,128)(2,1)S(1)}, bf16[128,1024]{0,1:T(8,128)(2,1)S(1)}, u32[]{:S(2)}, u32[]{:S(2)}) collective-permute-start(bf16[128,1024]{0,1:T(8,128)(2,1)S(1)} %get-tuple-element.29), channel_id=1, source_target_pairs={{0,1},{1,2},{2,3},{4,5},{5,6},{6,7},{8,9},{9,10},{10,11},{12,13},{... | collective-permute-start | bytes 786440 | tf_op jit(solution)/shard_map/ppermute | solution.py:33
  111.2 1.3 collective-permute-start.5
  113.2 1.5 collective-permute-done.5
  121.4 6.2 %collective-permute-start.6 = (bf16[128,1024]{0,1:T(8,128)(2,1)S(1)}, bf16[128,1024]{0,1:T(8,128)(2,1)S(1)}, u32[]{:S(2)}, u32[]{:S(2)}) collective-permute-start(bf16[128,1024]{0,1:T(8,128)(2,1)S(1)} %get-tuple-element.27), channel_id=1, source_target_pairs={{0,1},{1,2},{2,3},{4,5},{5,6},{6,7},{8,9},{9,10},{10,11},{12,13},{... | collective-permute-start | bytes 786440 | tf_op jit(solution)/shard_map/ppermute | solution.py:33
  127.6 1.3 collective-permute-start.7
  129.3 1.7 collective-permute-done.7
  131.5 1.8 fusion.36
  134.7 1.3 fusion.4
  136.0 1.4 fusion.7
  140.6 2.3 pad_maximum_fusion
  142.9 35.8 %all-gather.2.cloned.1.call-done = bf16[8,2,32,1024]{3,2,1,0:T(8,128)(2,1)} async-done(((bf16[1,2,32,1024]{3,2,1,0:T(8,128)(2,1)}), bf16[8,2,32,1024]{3,2,1,0:T(8,128)(2,1)}) %all-gather.2.cloned.1.call-update) | async-done | bytes 1048592 | tf_op jit(solution)/shard_map/all_gather | solution.py:200
  178.8 2.1 reduce_sum.324
  180.9 88.5 %reduce-scatter.6.cloned.1.call-done = bf16[2,4,64,512]{3,2,1,0:T(8,128)(2,1)} async-done(((bf16[2,4,512,512]{3,2,1,0:T(8,128)(2,1)}), bf16[2,4,64,512]{3,2,1,0:T(8,128)(2,1)}) %reduce-scatter.6.cloned.1.call-update) | async-done | bytes 524304 | tf_op jit(solution)/shard_map/reduce_scatter | solution.py:196
  269.5 1.6 copy.13
  271.1 1.4 reshape.399
  273.5 18.2 %reduce-scatter.8.cloned.1.call-done = bf16[2,32,256]{2,1,0:T(8,128)(2,1)} async-done(((bf16[2,32,1024]{2,1,0:T(8,128)(2,1)}), bf16[2,32,256]{2,1,0:T(8,128)(2,1)}) %reduce-scatter.8.cloned.1.call-update) | async-done | bytes 32784 | tf_op jit(solution)/shard_map/reduce_scatter | solution.py:204
  291.8 1.4 convert_element_type.216
  293.2 22.6 %reduce-scatter.10.cloned.1.call-done = bf16[128,512]{1,0:T(8,128)(2,1)} async-done(((bf16[512,512]{1,0:T(8,128)(2,1)}), bf16[128,512]{1,0:T(8,128)(2,1)}) %reduce-scatter.10.cloned.1.call-update) | async-done | bytes 131088
  315.8 1.1 reshape.400
  (199 shorter events, 31.3 us)
Async XLA Ops:
  7.2 5.9 %copy-start = (bf16[1,256,512]{2,1,0:T(8,128)(2,1)S(1)}, bf16[1,256,512]{2,1,0:T(8,128)(2,1)}, u32[]{:S(2)}) copy-start(bf16[1,256,512]{2,1,0:T(8,128)(2,1)} %param.7) | copy-start | bytes 786436
  7.2 171.6 %all-gather.2.cloned.1.call-start = ((), (), s32[]{:S(2)}) async-start(), calls=%async_computation.4 | async-start | bytes 1179648 | tf_op jit(solution)/shard_map/all_gather | solution.py:200
  11.4 66.2 %copy-start.26 = (f32[512]{0:T(512)}, f32[512]{0:T(512)S(1)}, u32[]{:S(2)}) copy-start(f32[512]{0:T(512)S(1)} %get-tuple-element.48) | copy-start | bytes 6148
  11.4 6.9 %copy-start.3 = (f32[2,32,1024]{2,1,0:T(8,128)S(1)}, f32[2,32,1024]{2,1,0:T(8,128)}, u32[]{:S(2)}) copy-start(f32[2,32,1024]{2,1,0:T(8,128)} %param.13) | copy-start | bytes 786436
  11.4 7.1 %copy-start.24 = (s32[256,32]{0,1:T(8,128)S(1)}, s32[256,32]{0,1:T(8,128)}, u32[]{:S(2)}) copy-start(s32[256,32]{0,1:T(8,128)} %param.10) | copy-start | bytes 98308
  11.4 7.2 %copy-start.31 = (s32[2]{0:T(128)S(1)}, s32[2]{0:T(128)}, u32[]{:S(2)}) copy-start(s32[2]{0:T(128)} %constant.75) | copy-start | bytes 28
  11.5 7.2 %copy-start.30 = (s32[2]{0:T(128)S(1)}, s32[2]{0:T(128)}, u32[]{:S(2)}) copy-start(s32[2]{0:T(128)} %constant.72) | copy-start | bytes 28
  11.5 7.3 %copy-start.25 = (s32[256,32]{0,1:T(8,128)S(1)}, s32[256,32]{0,1:T(8,128)}, u32[]{:S(2)}) copy-start(s32[256,32]{0,1:T(8,128)} %param.11) | copy-start | bytes 98308
  13.1 6.1 %copy-start.4 = (bf16[1,256,512]{2,1,0:T(8,128)(2,1)S(1)}, bf16[1,256,512]{2,1,0:T(8,128)(2,1)}, u32[]{:S(2)}) copy-start(bf16[1,256,512]{2,1,0:T(8,128)(2,1)} %param.8) | copy-start | bytes 786436
  14.6 64.4 %collective-permute-start = (bf16[128,1024]{1,0:T(8,128)(2,1)S(1)}, bf16[128,1024]{1,0:T(8,128)(2,1)S(1)}, u32[]{:S(2)}, u32[]{:S(2)}) collective-permute-start(bf16[128,1024]{1,0:T(8,128)(2,1)S(1)} %get-tuple-element.33), channel_id=1, source_target_pairs={{0,1},{1,2},{2,3},{4,5},{5,6},{6,7},{8,9},{9,10},{10,11},{12,13},{... | collective-permute-start | bytes 786440 | tf_op jit(solution)/shard_map/ppermute | solution.py:21
  17.0 62.0 %collective-permute-start.1 = (bf16[128,1024]{1,0:T(8,128)(2,1)S(1)}, bf16[128,1024]{1,0:T(8,128)(2,1)S(1)}, u32[]{:S(2)}, u32[]{:S(2)}) collective-permute-start(bf16[128,1024]{1,0:T(8,128)(2,1)S(1)} %get-tuple-element.34), channel_id=1, source_target_pairs={{1,0},{2,1},{3,2},{5,4},{6,5},{7,6},{9,8},{10,9},{11,10},{13,12},{... | collective-permute-start | bytes 786440 | tf_op jit(solution)/shard_map/ppermute | solution.py:23
  85.0 7.0 %collective-permute-start.2 = (bf16[128,1024]{1,0:T(8,128)(2,1)S(1)}, bf16[128,1024]{1,0:T(8,128)(2,1)S(1)}, u32[]{:S(2)}, u32[]{:S(2)}) collective-permute-start(bf16[128,1024]{1,0:T(8,128)(2,1)S(1)} %get-tuple-element.31), channel_id=1, source_target_pairs={{0,1},{1,2},{2,3},{4,5},{5,6},{6,7},{8,9},{9,10},{10,11},{12,13},{... | collective-permute-start | bytes 786440 | tf_op jit(solution)/shard_map/ppermute | solution.py:21
  90.1 4.7 %collective-permute-start.3 = (bf16[128,1024]{1,0:T(8,128)(2,1)S(1)}, bf16[128,1024]{1,0:T(8,128)(2,1)S(1)}, u32[]{:S(2)}, u32[]{:S(2)}) collective-permute-start(bf16[128,1024]{1,0:T(8,128)(2,1)S(1)} %get-tuple-element.32), channel_id=1, source_target_pairs={{1,0},{2,1},{3,2},{5,4},{6,5},{7,6},{9,8},{10,9},{11,10},{13,12},{... | collective-permute-start | bytes 786440 | tf_op jit(solution)/shard_map/ppermute | solution.py:23
  102.6 10.2 %copy-start.6 = (bf16[256,128]{0,1:T(8,128)(2,1)}, bf16[256,128]{0,1:T(8,128)(2,1)S(1)}, u32[]{:S(2)}) copy-start(bf16[256,128]{0,1:T(8,128)(2,1)S(1)} %convolution_convert_fusion.25) | copy-start | bytes 196612
  104.5 8.6 %collective-permute-start.4 = (bf16[128,1024]{0,1:T(8,128)(2,1)S(1)}, bf16[128,1024]{0,1:T(8,128)(2,1)S(1)}, u32[]{:S(2)}, u32[]{:S(2)}) collective-permute-start(bf16[128,1024]{0,1:T(8,128)(2,1)S(1)} %get-tuple-element.29), channel_id=1, source_target_pairs={{0,1},{1,2},{2,3},{4,5},{5,6},{6,7},{8,9},{9,10},{10,11},{12,13},{... | collective-permute-start | bytes 786440 | tf_op jit(solution)/shard_map/ppermute | solution.py:33
  111.2 3.4 %collective-permute-start.5 = (bf16[128,1024]{0,1:T(8,128)(2,1)S(1)}, bf16[128,1024]{0,1:T(8,128)(2,1)S(1)}, u32[]{:S(2)}, u32[]{:S(2)}) collective-permute-start(bf16[128,1024]{0,1:T(8,128)(2,1)S(1)} %get-tuple-element.30), channel_id=1, source_target_pairs={{1,0},{2,1},{3,2},{5,4},{6,5},{7,6},{9,8},{10,9},{11,10},{13,12},{... | collective-permute-start | bytes 786440 | tf_op jit(solution)/shard_map/ppermute | solution.py:33
  118.1 10.8 %copy-start.8 = (bf16[256,128]{0,1:T(8,128)(2,1)}, bf16[256,128]{0,1:T(8,128)(2,1)S(1)}, u32[]{:S(2)}) copy-start(bf16[256,128]{0,1:T(8,128)(2,1)S(1)} %convolution_convert_fusion.23) | copy-start | bytes 196612
  118.7 10.1 %copy-start.10 = (bf16[256,128]{0,1:T(8,128)(2,1)}, bf16[256,128]{0,1:T(8,128)(2,1)S(1)}, u32[]{:S(2)}) copy-start(bf16[256,128]{0,1:T(8,128)(2,1)S(1)} %convolution_convert_fusion.20) | copy-start | bytes 196612
  119.1 9.7 %copy-start.12 = (bf16[256,128]{0,1:T(8,128)(2,1)}, bf16[256,128]{0,1:T(8,128)(2,1)S(1)}, u32[]{:S(2)}) copy-start(bf16[256,128]{0,1:T(8,128)(2,1)S(1)} %convolution_convert_fusion.21) | copy-start | bytes 196612
  119.6 9.4 %copy-start.14 = (bf16[256,128]{0,1:T(8,128)(2,1)}, bf16[256,128]{0,1:T(8,128)(2,1)S(1)}, u32[]{:S(2)}) copy-start(bf16[256,128]{0,1:T(8,128)(2,1)S(1)} %convolution_convert_fusion.22) | copy-start | bytes 196612
  121.4 7.9 %collective-permute-start.6 = (bf16[128,1024]{0,1:T(8,128)(2,1)S(1)}, bf16[128,1024]{0,1:T(8,128)(2,1)S(1)}, u32[]{:S(2)}, u32[]{:S(2)}) collective-permute-start(bf16[128,1024]{0,1:T(8,128)(2,1)S(1)} %get-tuple-element.27), channel_id=1, source_target_pairs={{0,1},{1,2},{2,3},{4,5},{5,6},{6,7},{8,9},{9,10},{10,11},{12,13},{... | collective-permute-start | bytes 786440 | tf_op jit(solution)/shard_map/ppermute | solution.py:33
  127.6 3.4 %collective-permute-start.7 = (bf16[128,1024]{0,1:T(8,128)(2,1)S(1)}, bf16[128,1024]{0,1:T(8,128)(2,1)S(1)}, u32[]{:S(2)}, u32[]{:S(2)}) collective-permute-start(bf16[128,1024]{0,1:T(8,128)(2,1)S(1)} %get-tuple-element.28), channel_id=1, source_target_pairs={{1,0},{2,1},{3,2},{5,4},{6,5},{7,6},{9,8},{10,9},{11,10},{13,12},{... | collective-permute-start | bytes 786440 | tf_op jit(solution)/shard_map/ppermute | solution.py:33
  134.1 135.3 %reduce-scatter.6.cloned.1.call-start = ((), (), s32[]{:S(2)}) async-start(), calls=%async_computation.3 | async-start | bytes 4718592 | tf_op jit(solution)/shard_map/reduce_scatter | solution.py:196
  134.7 3.5 %copy-start.17 = (bf16[256,128]{0,1:T(8,128)(2,1)S(1)}, bf16[256,128]{0,1:T(8,128)(2,1)}, u32[]{:S(2)}) copy-start(bf16[256,128]{0,1:T(8,128)(2,1)} %copy-done.16) | copy-start | bytes 196612
  134.7 3.5 %copy-start.19 = (bf16[256,128]{0,1:T(8,128)(2,1)S(1)}, bf16[256,128]{0,1:T(8,128)(2,1)}, u32[]{:S(2)}) copy-start(bf16[256,128]{0,1:T(8,128)(2,1)} %copy-done.18) | copy-start | bytes 196612
  134.7 3.5 %copy-start.21 = (bf16[256,128]{0,1:T(8,128)(2,1)S(1)}, bf16[256,128]{0,1:T(8,128)(2,1)}, u32[]{:S(2)}) copy-start(bf16[256,128]{0,1:T(8,128)(2,1)} %copy-done.20) | copy-start | bytes 196612
  134.7 3.5 %copy-start.23 = (bf16[256,128]{0,1:T(8,128)(2,1)S(1)}, bf16[256,128]{0,1:T(8,128)(2,1)}, u32[]{:S(2)}) copy-start(bf16[256,128]{0,1:T(8,128)(2,1)} %copy-done.22) | copy-start | bytes 196612
  142.9 148.9 %reduce-scatter.8.cloned.1.call-start = ((), (), s32[]{:S(2)}) async-start(), calls=%async_computation.5 | async-start | bytes 163840 | tf_op jit(solution)/shard_map/reduce_scatter | solution.py:204
  180.9 91.7 %copy-start.29 = (f32[256]{0:T(256)S(1)}, f32[256]{0:T(256)}, u32[]{:S(2)}) copy-start(f32[256]{0:T(256)} %get-tuple-element.6) | copy-start | bytes 3076
  180.9 91.7 %copy-start.28 = (f32[256]{0:T(256)S(1)}, f32[256]{0:T(256)}, u32[]{:S(2)}) copy-start(f32[256]{0:T(256)} %get-tuple-element.7) | copy-start | bytes 3076
  180.9 91.7 %copy-start.1 = (f32[256,512]{1,0:T(8,128)S(1)}, f32[256,512]{1,0:T(8,128)}, u32[]{:S(2)}) copy-start(f32[256,512]{1,0:T(8,128)} %get-tuple-element.79) | copy-start | bytes 1572868
  180.9 134.9 %reduce-scatter.10.cloned.1.call-start = ((), (), s32[]{:S(2)}) async-start(), calls=%async_computation.6 | async-start | bytes 655360
  (12 other events, 24.4 us)
Sparse Core Ops, SparseCore 0:
  134.3 44.4 all-gather.1
  182.4 87.0 reduce-scatter.5
  272.5 19.2 reduce-scatter.7
  294.1 21.6 reduce-scatter.9
